TPU v7x, 32 devices: a whole 2x2x4 slice. The times are simulated.
32 devices in a mesh: rows: 8 (over y, x, core), cols: 4 (over z).
Axes of the slice: x: 2, y: 2, z: 4, core: 2. Of those that a mesh axis runs over, the one named last changes fastest.
Arguments:
- latent: float32 [1, 512, 512, 128], P(None, 'rows', 'cols'), may hold values from -6 to 6
- w_small: float32 [512, 128], replicated, may hold values from -0.25 to 0.25
- w_large: float32 [2048, 128], replicated, may hold values from -0.125 to 0.125
- gain_embed: float32 [256], replicated, may hold values from 0.1 to 1.9
- gain_attn: float32 [256], replicated, may hold values from 0.1 to 1.9
- w_qkv: float32 [256, 768], replicated, may hold values from -8 to 8
- pos_bias: float32 [8, 16, 16], replicated, may hold values from -4 to 4
- w_proj: float32 [256, 256], replicated, may hold values from -0.375 to 0.375
- gain_mlp: float32 [256], replicated, may hold values from 0.1 to 1.9
- w_up: float32 [256, 1024], replicated, may hold values from -0.375 to 0.375
- w_down: float32 [1024, 256], replicated, may hold values from -0.1875 to 0.1875
Outputs:
- result: float32 [1, 256, 256, 256], P(None, 'rows', 'cols')
All inputs are finite; a program needn't handle non-finite values.
Results may differ from a plain program's by a relative error of at most 0.0003.
Values sent between devices are 32-bit elements; how exact they have to be, the bound alone decides.
A program may use at most 192 MiB of HBM per device.

v0:
```python
import jax
import jax.numpy as jnp
from jax import lax
from jax.sharding import PartitionSpec as P

HEADS = 8


def padded_2(block, sides, width):
    for axis, dim in sides:
        count = lax.axis_size(axis)
        forward = [(i, i + 1) for i in range(count - 1)]
        backward = [(target, source) for source, target in forward]
        low = lax.ppermute(
            lax.slice_in_dim(block, block.shape[dim] - width, None, axis=dim), axis, forward
        )
        high = lax.ppermute(lax.slice_in_dim(block, 0, width, axis=dim), axis, backward)
        block = jnp.concatenate([low, block, high], axis=dim)
    return block


def matmul(left, right):
    return jnp.dot(left, right, precision=lax.Precision.HIGHEST, preferred_element_type=jnp.float32)


def layer_norm(values, gain):
    center = values - jnp.mean(values, axis=-1, keepdims=True)
    spread = jnp.mean(center * center, axis=-1, keepdims=True)
    return center * lax.rsqrt(spread + 1e-05) * gain


def attend(qkv_groups, pos_bias):
    groups, members, triple = qkv_groups.shape
    width = triple // 3
    head_width = width // HEADS
    split = qkv_groups.reshape(groups, members, 3, HEADS, head_width)
    scale = 1.0 / jnp.sqrt(jnp.float32(head_width))
    scores = (
        jnp.einsum(
            "gqhd,gkhd->ghqk", split[:, :, 0], split[:, :, 1], precision=lax.Precision.HIGHEST
        )
        * scale
        + pos_bias[None]
    )
    top = jnp.max(scores, axis=-1, keepdims=True)
    expd = jnp.exp(scores - top)
    probs = expd / jnp.sum(expd, axis=-1, keepdims=True)
    mixed = jnp.einsum("ghqk,gkhd->gqhd", probs, split[:, :, 2], precision=lax.Precision.HIGHEST)
    return mixed.reshape(groups * members, width)


def feed_forward(after, gain_mlp, w_up, w_down):
    hidden = jax.nn.gelu(matmul(layer_norm(after, gain_mlp), w_up), approximate=False)
    return after + matmul(hidden, w_down)


def to_groups(flat):
    row_count = lax.axis_size("rows")
    col_count = lax.axis_size("cols")
    features = flat.shape[-1]
    slots = flat.shape[0] // (row_count * col_count)
    moved = lax.all_to_all(
        lax.all_to_all(
            flat.reshape(row_count, col_count, slots, features),
            "rows",
            split_axis=0,
            concat_axis=0,
            tiled=True,
        ),
        "cols",
        split_axis=1,
        concat_axis=1,
        tiled=True,
    )
    moved = moved.reshape(row_count // 2, 2, col_count, slots, features).transpose(1, 3, 0, 2, 4)
    return moved.reshape(2 * slots, row_count // 2 * col_count, features)


def to_tiles(grouped):
    row_count = lax.axis_size("rows")
    col_count = lax.axis_size("cols")
    features = grouped.shape[-1]
    slots = grouped.shape[0] // 2
    ordered = grouped.reshape(2, slots, row_count // 2, col_count, features).transpose(
        2, 0, 3, 1, 4
    )
    moved = lax.all_to_all(
        lax.all_to_all(
            ordered.reshape(row_count, col_count, slots, features),
            "rows",
            split_axis=0,
            concat_axis=0,
            tiled=True,
        ),
        "cols",
        split_axis=1,
        concat_axis=1,
        tiled=True,
    )
    return moved.reshape(row_count * col_count * slots, features)


def per_device(
    latent, w_small, w_large, gain_embed, gain_attn, w_qkv, pos_bias, w_proj, gain_mlp, w_up, w_down
):
    samples, height, width, channels = latent.shape
    rows_tile = height // 2
    cols_tile = width // 2
    embed_width = w_small.shape[1]
    blocked = latent.reshape(samples, rows_tile, 2, cols_tile, 2, channels)
    kernel_small = w_small.reshape(2, 2, channels, embed_width)
    small = jnp.einsum(
        "nipjqc,pqce->nije",
        blocked,
        kernel_small,
        precision=lax.Precision.HIGHEST,
        preferred_element_type=jnp.float32,
    ).reshape(-1, embed_width)
    padded = padded_2(latent, (("rows", 1), ("cols", 2)), 1)
    padded_blocks = padded.reshape(samples, rows_tile + 1, 2, cols_tile + 1, 2, channels)
    kernel_large = w_large.reshape(2, 2, 2, 2, channels, embed_width)
    large = jnp.zeros((samples, rows_tile, cols_tile, embed_width), jnp.float32)
    for row_block in range(2):
        for col_block in range(2):
            piece = padded_blocks[
                :, row_block : row_block + rows_tile, :, col_block : col_block + cols_tile
            ]
            large = large + jnp.einsum(
                "nipjqc,pqce->nije",
                piece,
                kernel_large[row_block, :, col_block],
                precision=lax.Precision.HIGHEST,
                preferred_element_type=jnp.float32,
            )
    large = large.reshape(-1, embed_width)
    embedded = layer_norm(jnp.concatenate([small, large], axis=-1), gain_embed)
    features = embedded.shape[-1]
    grouped = to_groups(embedded)
    groups_count, members, _ = grouped.shape
    tokens = grouped.reshape(-1, features)
    qkv = matmul(layer_norm(tokens, gain_attn), w_qkv)
    mixed = attend(qkv.reshape(groups_count, members, 3 * features), pos_bias)
    after = tokens + matmul(mixed, w_proj)
    finished = feed_forward(after, gain_mlp, w_up, w_down)
    output = to_tiles(finished.reshape(groups_count, members, features))
    return output.reshape(samples, rows_tile, cols_tile, features)


def solution(mesh):
    in_specs = (P(None, "rows", "cols", None), P(), P(), P(), P(), P(), P(), P(), P(), P(), P())
    out_specs = P(None, "rows", "cols", None)
    return jax.shard_map(
        per_device, mesh=mesh, in_specs=in_specs, out_specs=out_specs, check_vma=False
    )
```

profile of v0, /device:TPU:0, one launch (start us, length us, event | category | flops | bytes accessed | tf_op | source)
XLA Modules:
  0.0 375.0 jit_solution(15170629082405868763)
XLA Ops:
  0.0 1.0 fusion.159
  1.0 2.5 collective-permute-start
  3.6 1.3 collective-permute-start.1
  4.9 0.0 copy-start.7
  4.9 2.8 copy.87
  7.7 0.0 collective-permute-done
  7.7 0.5 constant_dynamic-update-slice_fusion.1
  8.2 0.6 collective-permute-done.1
  8.9 3.7 collective-permute-start.2
  12.6 1.3 collective-permute-start.3
  13.9 0.0 copy-done.7
  13.9 3.5 bitcast_reduce_fusion
  17.5 0.1 reduce_sum.84
  17.6 0.0 collective-permute-done.2
  17.6 0.9 collective-permute-done.3
  18.5 4.7 %pad_maximum_fusion = f32[1,66,130,128]{3,2,1,0:T(8,128)} fusion(f32[1,66,1,128]{3,2,1,0:T(1,128)S(1)} %collective-permute-done.3, f32[1,66,128,128]{3,2,1,0:T(8,128)} %copy-done.3, f32[1,66,1,128]{3,2,1,0:T(1,128)S(1)} %collective-permute-done.2), kind=kLoop, calls=%fused_computation.70 | loop fusion | flops 2196480 | bytes 8785920 | tf_op jit(solution)/shard_map/concatenate | solution.py:18
  23.2 7.2 %reshape.172 = f32[1,33,2,65,2,128]{5,0,4,3,2,1:T(1,128)} reshape(f32[1,66,130,128]{3,2,1,0:T(8,128)} %pad_maximum_fusion) | data formatting | bytes 8785920 | tf_op jit(solution)/shard_map/reshape | solution.py:120
  30.4 15.0 %fusion.157 = (f32[1,32,2,64,2,128]{5,0,4,3,2,1:T(1,128)S(1)}, f32[1,32,2,64,2,128]{5,0,4,3,2,1:T(1,128)S(1)}, f32[1,32,2,64,2,128]{5,0,4,3,2,1:T(1,128)S(1)}, f32[1,32,2,64,2,128]{5,0,4,3,2,1:T(1,128)S(1)}) fusion(f32[1,33,2,65,2,128]{5,0,4,3,2,1:T(1,128)} %reshape.172), kind=kLoop, calls=%fused_computation.190 | loop fusion | bytes 33554432 | tf_op jit(solution)/shard_map/slice | solution.py:125
  45.4 0.0 copy-done.5
  45.5 3.5 fusion.117
  49.0 3.5 fusion.116
  52.5 0.0 copy-start.10
  52.5 3.5 fusion.118
  56.1 3.8 %fusion.160 = (f32[32,64]{1,0:T(8,128)S(1)}, f32[32,64,128]{2,1,0:T(8,128)S(1)}) fusion(f32[32,64,128]{2,1,0:T(8,128)S(1)} %fusion.118, f32[32,64,128]{2,1,0:T(8,128)S(1)} %fusion.117, f32[32,64,128]{2,1,0:T(8,128)S(1)} %fusion.116, f32[2,2,2,2,128,128]{5,4,3,2,1,0:T(8,128)S(1)} %bitcast.167, f32[1,32,2,64,2,128]{5,0,4,3,2,1:T(1,128)S(1)} %get-tuple-element.8), kind=kOutput, calls=%fused_computation.193 | convolution fusion | flops 1611659264 | bytes 8658944 | tf_op jit(solution)/shard_map/nipjqc,pqce->nije/dot_general | solution.py:128
  59.9 0.1 reduce_sum.88
  60.0 0.6 fusion.110
  60.6 0.1 rsqrt.29
  60.7 0.0 copy-start.8
  60.7 0.7 fusion.108
  61.5 32.6 %all_to_all.20 = f32[8,4,64,256]{3,2,1,0:T(8,128)S(1)} all-to-all(f32[8,4,64,256]{3,2,1,0:T(8,128)S(1)} %fusion.108), channel_id=1, replica_groups=mesh['rows'=8,'cols'=4] {'rows'}, dimensions={0} | all-to-all | bytes 4194304 | tf_op jit(solution)/shard_map/all_to_all | solution.py:63
  94.1 1.5 copy.96
  95.5 5.0 %all-to-all-start.1 = ((f32[8,4,64,256]{3,2,0,1:T(8,128)}), f32[8,4,64,256]{3,2,0,1:T(8,128)S(1)}, u32[]{:S(2)}, u32[]{:S(2)}) async-start(f32[8,4,64,256]{3,2,0,1:T(8,128)} %copy.96), calls=%async_computation.1 | async-start | bytes 4194304 | tf_op jit(solution)/shard_map/all_to_all | solution.py:62
  100.6 0.1 copy.102
  100.7 2.3 copy.99
  103.0 45.3 %all-to-all-done.1 = f32[8,4,64,256]{3,2,0,1:T(8,128)S(1)} async-done(((f32[8,4,64,256]{3,2,0,1:T(8,128)}), f32[8,4,64,256]{3,2,0,1:T(8,128)S(1)}, u32[]{:S(2)}, u32[]{:S(2)}) %all-to-all-start.1) | async-done | bytes 2097184 | tf_op jit(solution)/shard_map/all_to_all | solution.py:62
  148.2 1.6 fusion.156
  149.8 2.7 copy.159
  152.5 0.1 broadcast_multiply_fusion
  152.6 1.9 multiply_reduce_fusion.1
  154.5 0.8 add_rsqrt_fusion
  155.3 3.0 reshape_reshape.10
  158.3 3.5 multiply_multiply_fusion.5
  161.8 1.2 copy.98
  163.0 5.6 %fusion.162 = f32[128,16,3,8,32]{0,4,3,2,1:T(8,128)S(1)} fusion(f32[128,16,256,1,1]{2,0,4,3,1:T(8,128)S(1)} %bitcast.162, f32[3,8,32,256,1]{3,2,1,0,4:T(8,128)S(1)} %bitcast.163), kind=kOutput, calls=%fused_computation.195 | convolution fusion | flops 4831838208 | bytes 9175040 | tf_op jit(solution)/shard_map/dot_general | solution.py:23
  168.6 2.7 slice_bitcast_fusion
  171.4 8.4 %copy.101 = f32[128,16,8,32]{3,1,2,0:T(8,128)} copy(f32[128,16,8,32]{0,3,2,1:T(8,128)} %get-tuple-element.5) | data formatting | bytes 4194304 | tf_op jit(solution)/shard_map/squeeze | solution.py:40
  179.8 8.5 %copy.100 = f32[128,16,8,32]{3,1,2,0:T(8,128)} copy(f32[128,16,8,32]{0,3,2,1:T(8,128)} %get-tuple-element.6) | data formatting | bytes 4194304 | tf_op jit(solution)/shard_map/squeeze | solution.py:40
  188.3 7.6 %copy.103 = f32[128,16,8,32]{3,1,2,0:T(8,128)} copy(f32[128,16,8,32]{0,3,2,1:T(8,128)S(1)} %get-tuple-element.7) | data formatting | bytes 4194304 | tf_op jit(solution)/shard_map/squeeze | solution.py:48
  195.8 17.9 %fusion.61 = (f32[128,8,16]{2,1,0:T(8,128)S(1)}, f32[128,8,16,16]{2,3,1,0:T(8,128)S(1)}) fusion(f32[8,16,16]{1,2,0:T(8,128)S(1)} %copy.102, f32[128,16,8,32]{3,1,2,0:T(8,128)} %copy.100, f32[128,16,8,32]{3,1,2,0:T(8,128)} %copy.101), kind=kOutput, calls=%fused_computation.68 | convolution fusion | flops 101433344 | bytes 5316608 | tf_op jit(solution)/shard_map/gqhd,gkhd->ghqk/dot_general | solution.py:39
  213.7 5.5 %fusion.62 = f32[128,8,16]{2,1,0:T(8,128)S(1)} fusion(f32[128,8,16,16]{2,3,1,0:T(8,128)S(1)} %get-tuple-element.21, f32[128,8,16]{2,1,0:T(8,128)S(1)} %get-tuple-element.20, f32[8,16,16]{1,2,0:T(8,128)S(1)} %copy.102), kind=kLoop, calls=%fused_computation.69 | loop fusion | flops 1032192 | bytes 1187840 | tf_op jit(solution)/shard_map/reduce_sum | solution.py:47
  219.2 15.9 %fusion.101 = f32[128,16,8,32]{3,1,2,0:T(8,128)S(1)} fusion(f32[128,16,8,32]{3,1,2,0:T(8,128)S(1)} %copy-done.2, f32[128,8,16,16]{2,3,1,0:T(8,128)S(1)} %get-tuple-element.21, f32[128,8,16]{2,1,0:T(8,128)S(1)} %fusion.62, f32[128,8,16]{2,1,0:T(8,128)S(1)} %get-tuple-element.20, f32[8,16,16]{1,2,0:T(8,128)S(1)} %copy.102), kind=kOutput, calls=%fused_computation.113 | convolution fusion | flops 101711872 | bytes 5382144 | tf_op jit(solution)/shard_map/ghqk,gkhd->gqhd/dot_general | solution.py:48
  235.2 7.3 %copy.105 = f32[128,16,8,32]{3,2,1,0:T(8,128)} copy(f32[128,16,8,32]{3,1,2,0:T(8,128)S(1)} %fusion.101) | data formatting | bytes 4194304 | tf_op jit(solution)/shard_map/ghqk,gkhd->gqhd/transpose | solution.py:48
  242.5 6.1 %reshape.180 = f32[2048,256]{1,0:T(8,128)S(1)} reshape(f32[128,16,8,32]{3,2,1,0:T(8,128)} %copy.105) | data formatting | bytes 4194304 | tf_op jit(solution)/shard_map/reshape | solution.py:49
  248.6 3.6 fusion.161
  252.2 0.6 multiply_reduce_fusion
  252.9 0.0 copy-start.12
  252.9 7.5 %fusion.111 = f32[2048,1024]{1,0:T(8,128)S(1)} fusion(f32[256,1024]{1,0:T(8,128)S(1)} %copy-done, f32[2048,256]{1,0:T(8,128)S(1)} %get-tuple-element.23, f32[256]{0:T(256)S(1)} %copy-done.9, f32[2048]{0:T(1024)S(1)} %add_rsqrt_fusion.1, f32[2048]{0:T(1024)S(1)} %broadcast_multiply_fusion.1), kind=kOutput, calls=%fused_computation.126 | convolution fusion | flops 6444023808 | bytes 11551744 | tf_op jit(solution)/shard_map/dot_general | solution.py:23
  260.4 30.2 %fusion.104 = f32[2048,256]{1,0:T(8,128)} fusion(f32[2048,256]{1,0:T(8,128)S(1)} %get-tuple-element.23, f32[1024,256]{1,0:T(8,128)S(1)} %copy-done.12, f32[2048,1024]{1,0:T(8,128)S(1)} %fusion.111), kind=kOutput, calls=%fused_computation.115 | convolution fusion | flops 6577192960 | bytes 13631488 | tf_op jit(solution)/shard_map/dot_general | solution.py:23
  290.6 1.9 reshape_reshape.11
  292.5 1.2 copy.106
  293.7 29.0 %all_to_all.21 = f32[8,4,64,256]{3,2,1,0:T(8,128)S(1)} all-to-all(f32[8,4,64,256]{3,2,1,0:T(8,128)S(1)} %bitcast.161), channel_id=1, replica_groups=mesh['rows'=8,'cols'=4] {'rows'}, dimensions={0} | all-to-all | bytes 4194304 | tf_op jit(solution)/shard_map/all_to_all | solution.py:88
  322.7 0.2 copy.107
  323.0 50.4 %all_to_all.22 = f32[8,4,64,256]{3,2,0,1:T(8,128)S(1)} all-to-all(f32[8,4,64,256]{3,2,0,1:T(8,128)S(1)} %copy.107), channel_id=1, replica_groups=mesh['rows'=8,'cols'=4] {'cols'}, dimensions={1} | all-to-all | bytes 4194304 | tf_op jit(solution)/shard_map/all_to_all | solution.py:87
  373.3 1.5 copy.108
  (28 shorter events, 0.1 us)
Async XLA Ops:
  0.0 252.9 %copy-start = (f32[256,1024]{1,0:T(8,128)S(1)}, f32[256,1024]{1,0:T(8,128)}, u32[]{:S(2)}) copy-start(f32[256,1024]{1,0:T(8,128)} %param.20) | copy-start | bytes 3145732
  0.0 7.7 %copy-start.1 = (f32[1,64,128,128]{3,2,1,0:T(8,128)S(1)}, f32[1,64,128,128]{3,2,1,0:T(8,128)}, u32[]{:S(2)}) copy-start(f32[1,64,128,128]{3,2,1,0:T(8,128)} %param.11) | copy-start | bytes 12582916
  1.0 6.7 %collective-permute-start = (f32[1,1,128,128]{3,2,1,0:T(8,128)S(1)}, f32[1,1,128,128]{3,2,1,0:T(8,128)S(1)}, u32[]{:S(2)}, u32[]{:S(2)}) collective-permute-start(f32[1,1,128,128]{3,2,1,0:T(8,128)S(1)} %get-tuple-element.15), channel_id=1, source_target_pairs={{0,4},{4,8},{8,12},{12,16},{16,20},{20,24},{24,28},{1,5},{5,9},{9,... | collective-permute-start | bytes 196616 | tf_op jit(solution)/shard_map/ppermute | solution.py:14
  3.6 5.2 %collective-permute-start.1 = (f32[1,1,128,128]{3,2,1,0:T(8,128)S(1)}, f32[1,1,128,128]{3,2,1,0:T(8,128)S(1)}, u32[]{:S(2)}, u32[]{:S(2)}) collective-permute-start(f32[1,1,128,128]{3,2,1,0:T(8,128)S(1)} %get-tuple-element.14), channel_id=1, source_target_pairs={{4,0},{8,4},{12,8},{16,12},{20,16},{24,20},{28,24},{5,1},{9,5},{13... | collective-permute-start | bytes 196616 | tf_op jit(solution)/shard_map/ppermute | solution.py:17
  4.9 9.1 %copy-start.7 = (f32[512,128]{1,0:T(8,128)S(1)}, f32[512,128]{1,0:T(8,128)}, u32[]{:S(2)}) copy-start(f32[512,128]{1,0:T(8,128)} %param.12) | copy-start | bytes 786436
  8.8 8.6 %copy-start.3 = (f32[1,66,128,128]{3,2,1,0:T(8,128)}, f32[1,66,128,128]{3,2,1,0:T(8,128)S(1)}, u32[]{:S(2)}) copy-start(f32[1,66,128,128]{3,2,1,0:T(8,128)S(1)} %constant_dynamic-update-slice_fusion) | copy-start | bytes 12976132
  8.9 8.7 %collective-permute-start.2 = (f32[1,66,1,128]{3,2,1,0:T(1,128)S(1)}, f32[1,66,1,128]{3,2,1,0:T(1,128)S(1)}, u32[]{:S(2)}, u32[]{:S(2)}) collective-permute-start(f32[1,66,1,128]{3,2,1,0:T(1,128)S(1)} %get-tuple-element.12), channel_id=1, source_target_pairs={{0,1},{1,2},{2,3},{4,5},{5,6},{6,7},{8,9},{9,10},{10,11},{12,13},{... | collective-permute-start | bytes 101384 | tf_op jit(solution)/shard_map/ppermute | solution.py:14
  12.6 5.8 %collective-permute-start.3 = (f32[1,66,1,128]{3,2,1,0:T(1,128)S(1)}, f32[1,66,1,128]{3,2,1,0:T(1,128)S(1)}, u32[]{:S(2)}, u32[]{:S(2)}) collective-permute-start(f32[1,66,1,128]{3,2,1,0:T(1,128)S(1)} %get-tuple-element.13), channel_id=1, source_target_pairs={{1,0},{2,1},{3,2},{5,4},{6,5},{7,6},{9,8},{10,9},{11,10},{13,12},{... | collective-permute-start | bytes 101384 | tf_op jit(solution)/shard_map/ppermute | solution.py:17
  30.4 15.0 %copy-start.5 = (f32[2048,128]{1,0:T(8,128)S(1)}, f32[2048,128]{1,0:T(8,128)}, u32[]{:S(2)}) copy-start(f32[2048,128]{1,0:T(8,128)} %param.13) | copy-start | bytes 3145732
  52.5 8.2 %copy-start.10 = (f32[256]{0:T(256)S(1)}, f32[256]{0:T(256)}, u32[]{:S(2)}) copy-start(f32[256]{0:T(256)} %param.14) | copy-start | bytes 3076
  60.7 39.9 %copy-start.8 = (f32[8,16,16]{2,1,0:T(8,128)S(1)}, f32[8,16,16]{2,1,0:T(8,128)}, u32[]{:S(2)}) copy-start(f32[8,16,16]{2,1,0:T(8,128)} %param.17) | copy-start | bytes 24580
  95.5 52.7 %all-to-all-start.1 = ((f32[8,4,64,256]{3,2,0,1:T(8,128)}), f32[8,4,64,256]{3,2,0,1:T(8,128)S(1)}, u32[]{:S(2)}, u32[]{:S(2)}) async-start(f32[8,4,64,256]{3,2,0,1:T(8,128)} %copy.96), calls=%async_computation.1 | async-start | bytes 4194304 | tf_op jit(solution)/shard_map/all_to_all | solution.py:62
  100.6 57.7 %copy-start.11 = (f32[256]{0:T(256)S(1)}, f32[256]{0:T(256)}, u32[]{:S(2)}) copy-start(f32[256]{0:T(256)} %param.15) | copy-start | bytes 3076
  158.3 4.8 %copy-start.4 = (f32[256,768]{0,1:T(8,128)S(1)}, f32[256,768]{0,1:T(8,128)}, u32[]{:S(2)}) copy-start(f32[256,768]{0,1:T(8,128)} %copy.99) | copy-start | bytes 2359300
  213.7 5.5 %copy-start.2 = (f32[128,16,8,32]{3,1,2,0:T(8,128)S(1)}, f32[128,16,8,32]{3,1,2,0:T(8,128)}, u32[]{:S(2)}) copy-start(f32[128,16,8,32]{3,1,2,0:T(8,128)} %copy.103) | copy-start | bytes 6291460
  242.5 6.1 %copy-start.6 = (f32[256,256]{1,0:T(8,128)S(1)}, f32[256,256]{1,0:T(8,128)}, u32[]{:S(2)}) copy-start(f32[256,256]{1,0:T(8,128)} %param.18) | copy-start | bytes 786436
  242.5 10.4 %copy-start.9 = (f32[256]{0:T(256)S(1)}, f32[256]{0:T(256)}, u32[]{:S(2)}) copy-start(f32[256]{0:T(256)} %param.19) | copy-start | bytes 3076
  252.9 7.5 %copy-start.12 = (f32[1024,256]{1,0:T(8,128)S(1)}, f32[1024,256]{1,0:T(8,128)}, u32[]{:S(2)}) copy-start(f32[1024,256]{1,0:T(8,128)} %param.21) | copy-start | bytes 3145732
where the time goes:
time: 382 us; the launch traced here: 375 us
  blocking collectives  112 us (29%)
  matrix products  98.6 us (26%)
  local copies, waits for them, and re-layouts  82.9 us (22%)
  waiting for transfers between devices  46.8 us (12%)
  other arithmetic  20.2 us (5%)
  starting transfers between devices  13.9 us (4%)
    all_to_all x1, blocking collectives, to_tiles(): lax.all_to_all(lax.all_to_all(ordered.reshape(row_count, col_count, slots...  50.4 us
    dot_general x4, matrix products, matmul(): jnp.dot(left, right, precision=lax.Precision.HIGHEST, preferred_element_t...  46.9 us
    all_to_all x1, waiting for transfers between devices, to_groups(): lax.all_to_all(lax.all_to_all(flat.reshape(row_count, col_count, slots, f...  45.3 us
    all_to_all x1, blocking collectives, to_groups(): lax.all_to_all(flat.reshape(row_count, col_count, slots, features), 'rows...  32.6 us
    all_to_all x1, blocking collectives, to_tiles(): lax.all_to_all(ordered.reshape(row_count, col_count, slots, features), 'r...  29 us
    dot_general x1, matrix products, attend(): jnp.einsum('gqhd,gkhd->ghqk', split[:, :, 0], split[:, :, 1], precision=l...  17.9 us
    dot_general x1, matrix products, attend(): jnp.einsum('ghqk,gkhd->gqhd', probs, split[:, :, 2], precision=lax.Precis...  15.9 us
    slice x1, local copies, waits for them, and re-layouts, per_device(): padded_blocks[:, row_block:row_block + rows_tile, :, col_block:col_block...  15 us
  transfers between devices with their start and end apart: 5, of which 3 were waited for; matrix products, arithmetic and copies ran while one was open for 2% of the time, Pallas kernels for 0%

commit v1 on v0

v1 whole, which is shorter than its diff:
```python
import functools

import jax
import jax.numpy as jnp
from jax import lax
from jax.experimental import pallas as pl
from jax.experimental.pallas import tpu as pltpu
from jax.sharding import PartitionSpec as P

HEADS = 8
STAGES = 4
MESH = pl.DeviceIdType.MESH
F32 = jnp.float32
BF16 = jnp.bfloat16


def split(values):
    high = values.astype(BF16)
    return high, (values - high.astype(F32)).astype(BF16)


def dot(left, right, dims=((1,), (0,))):
    return lax.dot_general(left, right, (dims, ((), ())), preferred_element_type=F32)


def dot3(left, right, dims=((1,), (0,))):
    left_hi, left_lo = left
    right_hi, right_lo = right
    return (
        dot(left_hi, right_lo, dims) + dot(left_lo, right_hi, dims) + dot(left_hi, right_hi, dims)
    )


def layer_norm(values, gain):
    center = values - jnp.mean(values, axis=-1, keepdims=True)
    spread = jnp.mean(center * center, axis=-1, keepdims=True)
    return center * lax.rsqrt(spread + 1e-05) * gain


def gelu(values):
    return 0.5 * values * (1.0 + lax.erf(values * 0.7071067811865476))


def block_kernel(
    sizes,
    lat, w_small, w_large, gain_embed, gain_attn, w_qkv, pos_bias, w_proj, gain_mlp, w_up, w_down,
    out,
    eo_hi, eo_lo, oe_hi, oe_lo, wc, we, wo, wq, wp, wu, wd, bias,
    emb, recv, done, row_halo, col_halo, corner_halo, col_edge,
    halo_send, halo_recv, go_send, go_recv, back_send, back_recv,
):
    row_count, col_count, members, phases = sizes
    rows, cols, chan = lat.shape
    tile_rows, tile_cols = rows // 2, cols // 2
    feat = gain_embed.shape[1]
    half = feat // 2
    stage_rows = tile_rows // STAGES
    stage_tokens = stage_rows * tile_cols
    share = stage_tokens // members
    groups = max(8, min(share, 256 // members))
    tokens = members * groups
    head = feat // HEADS

    r = lax.axis_index("rows")
    c = lax.axis_index("cols")
    core = lax.rem(r, phases)
    me = (r // phases) * col_count + c

    def place(member):
        return (member // col_count) * phases + core, lax.rem(member, col_count)

    def other(step):
        return lax.rem(me + step, members)

    barrier = pltpu.get_barrier_semaphore()

    def greet(step, carry):
        pl.semaphore_signal(barrier, inc=1, device_id=place(other(step)), device_id_type=MESH)
        return carry

    lax.fori_loop(1, members, greet, 0)
    up, down = r > 0, r < row_count - 1
    west, east = c > 0, c < col_count - 1
    for row_ok, dr in ((up, -1), (down, 1)):
        for col_ok, dc in ((True, 0), (west, -1), (east, 1)):
            ok = row_ok if col_ok is True else jnp.logical_and(row_ok, col_ok)

            @pl.when(ok)
            def _(dr=dr, dc=dc):
                pl.semaphore_signal(barrier, inc=1, device_id=(r + dr, c + dc), device_id_type=MESH)

    col_edge[0] = lat[:, 0, :]
    col_edge[1] = lat[:, cols - 1, :]
    number = lambda flag: jnp.where(flag, 1, 0)
    vertical = number(up) + number(down)
    horizontal = 1 + number(west) + number(east)
    pl.semaphore_wait(barrier, members - 1 + vertical * horizontal)

    both = jnp.logical_and
    plan = [
        (up, down, (r - 1, c), lat.at[0], row_halo.at[1]),
        (down, up, (r + 1, c), lat.at[rows - 1], row_halo.at[0]),
        (west, east, (r, c - 1), col_edge.at[0], col_halo.at[1, pl.ds(8, rows)]),
        (east, west, (r, c + 1), col_edge.at[1], col_halo.at[0, pl.ds(8, rows)]),
        (both(up, west), both(down, east), (r - 1, c - 1), lat.at[0, pl.ds(0, 8)], corner_halo.at[3]),
        (both(up, east), both(down, west), (r - 1, c + 1), lat.at[0, pl.ds(cols - 8, 8)], corner_halo.at[2]),
        (both(down, west), both(up, east), (r + 1, c - 1), lat.at[rows - 1, pl.ds(0, 8)], corner_halo.at[1]),
        (both(down, east), both(up, west), (r + 1, c + 1), lat.at[rows - 1, pl.ds(cols - 8, 8)], corner_halo.at[0]),
    ]

    def halo_copy(index):
        _, _, target, source, destination = plan[index]
        return pltpu.make_async_remote_copy(
            src_ref=source, dst_ref=destination, send_sem=halo_send.at[index],
            recv_sem=halo_recv.at[index], device_id=target, device_id_type=MESH,
        )

    for index in range(8):
        @pl.when(plan[index][0])
        def _(index=index):
            halo_copy(index).start()

    def keep(ref, index, values):
        ref[(0,) + index], ref[(1,) + index] = split(values)

    for p in range(2):
        keep(wc, (p, slice(None), slice(0, half)), w_small[2 * p * chan : 2 * (p + 1) * chan])
        first = (p + 1) * 4 * chan + chan
        keep(wc, (p, slice(None), slice(half, feat)), w_large[first : first + 2 * chan])
        first = 3 * p * 4 * chan + chan
        keep(we, (p,), w_large[first : first + 2 * chan])
    for p in range(4):
        keep(wo, (p, slice(0, chan)), w_large[4 * p * chan : (4 * p + 1) * chan])
        keep(wo, (p, slice(chan, 2 * chan)), w_large[(4 * p + 3) * chan : (4 * p + 4) * chan])

    for index in range(8):
        _, arrives, _, _, destination = plan[index]

        @pl.when(arrives)
        def _(index=index):
            halo_copy(index).wait_recv()

        @pl.when(jnp.logical_not(arrives))
        def _(destination=destination):
            destination[...] = jnp.zeros(destination.shape, F32)

    for side, row in ((0, 7), (1, 0)):
        col_halo[side, 7] = corner_halo[side, row]
        col_halo[side, 8 + rows] = corner_halo[2 + side, row]

    first_row = lax.broadcasted_iota(jnp.int32, (tile_cols, 1), 0) == 0
    last_row = lax.broadcasted_iota(jnp.int32, (tile_cols, 1), 0) == tile_cols - 1

    def build(t, source):
        even = source[pl.ds(0, tile_cols, stride=2), :]
        odd = source[pl.ds(1, tile_cols, stride=2), :]
        before = jnp.where(first_row, col_halo[0, pl.ds(t + 7, 1)], pltpu.roll(odd, 1, 0))
        after = jnp.where(last_row, col_halo[1, pl.ds(t + 7, 1)], pltpu.roll(even, tile_cols - 1, 0))
        b, a = t % 2, t // 2
        for hi, lo, left, right in ((eo_hi, eo_lo, even, odd), (oe_hi, oe_lo, before, after)):
            hi[b, a, :, :chan], lo[b, a, :, :chan] = split(left)
            hi[b, a, :, chan:], lo[b, a, :, chan:] = split(right)

    build(0, row_halo.at[0])
    build(1, lat.at[0])
    build(rows + 1, row_halo.at[1])

    def go(s, member):
        rank = place(member)
        return pltpu.make_async_remote_copy(
            src_ref=emb.at[s, member], dst_ref=recv.at[s, me], send_sem=go_send.at[s, member],
            recv_sem=go_recv.at[s, me], device_id=rank, device_id_type=MESH,
        )

    def arrival(s, member):
        return pltpu.make_async_remote_copy(
            src_ref=emb.at[s, member], dst_ref=recv.at[s, member], send_sem=go_send.at[s, member],
            recv_sem=go_recv.at[s, member], device_id=place(member), device_id_type=MESH,
        )

    def home(s, owner):
        return out.at[pl.ds(pl.multiple_of(s * stage_tokens + owner * share, 8), share)]

    def back(s, member):
        return pltpu.make_async_remote_copy(
            src_ref=done.at[s, member], dst_ref=home(s, me), send_sem=back_send.at[s, member],
            recv_sem=back_recv.at[s, me], device_id=place(member), device_id_type=MESH,
        )

    def back_arrival(s, owner):
        return pltpu.make_async_remote_copy(
            src_ref=done.at[s, owner], dst_ref=home(s, owner), send_sem=back_send.at[s, owner],
            recv_sem=back_recv.at[s, owner], device_id=place(owner), device_id_type=MESH,
        )

    def own(s):
        return pltpu.make_async_copy(done.at[s, me], home(s, me), back_recv.at[s, me])

    def embed(s, carry):
        def line(t, inner):
            build(t, lat.at[t - 1])
            return inner

        first = 2 * stage_rows * s + 2
        lax.fori_loop(first, jnp.minimum(first + 2 * stage_rows, rows + 1), line, 0)

        def taps(hi, lo, p):
            where = (p % 2, pl.ds(stage_rows * s + p // 2, stage_rows))
            return tuple(ref[where].reshape(stage_tokens, 2 * chan) for ref in (hi, lo))

        def pair(ref, index):
            return ref[0, index], ref[1, index]

        wide = dot3(taps(eo_hi, eo_lo, 1), pair(wc, 0)) + dot3(taps(eo_hi, eo_lo, 2), pair(wc, 1))
        thin = dot3(taps(eo_hi, eo_lo, 0), pair(we, 0)) + dot3(taps(eo_hi, eo_lo, 3), pair(we, 1))
        for p in range(4):
            thin = thin + dot3(taps(oe_hi, oe_lo, p), pair(wo, p))
        joined = jnp.concatenate([wide[:, :half], wide[:, half:] + thin], axis=-1)
        emb[s] = layer_norm(joined, gain_embed[...]).reshape(members, share, feat)
        recv[s, me] = emb[s, me]

        def send(step, inner):
            go(s, other(step)).start()
            return inner

        lax.fori_loop(1, members, send, 0)
        return carry

    lax.fori_loop(0, STAGES, embed, 0)

    for ref, source in ((wq, w_qkv), (wp, w_proj), (wu, w_up), (wd, w_down)):
        ref[0], ref[1] = split(source[...])

    spread = (
        lax.broadcasted_iota(jnp.int32, (tokens, members), 0) // groups
        == lax.broadcasted_iota(jnp.int32, (tokens, members), 1)
    ).astype(F32)
    same = lax.rem(lax.broadcasted_iota(jnp.int32, (tokens, tokens), 0), groups) == lax.rem(
        lax.broadcasted_iota(jnp.int32, (tokens, tokens), 1), groups
    )
    exact = functools.partial(
        lax.dot_general, precision=lax.Precision.HIGHEST, preferred_element_type=F32
    )

    def widen(h, carry):
        tall = exact(spread, pos_bias[h], (((1,), (0,)), ((), ())))
        bias[h] = jnp.where(same, exact(tall, spread, (((1,), (1,)), ((), ()))), -1e30)
        return carry

    lax.fori_loop(0, HEADS, widen, 0)

    lane_head = lax.broadcasted_iota(jnp.int32, (1, feat), 1) // head
    scale = 1.0 / (head**0.5)

    def block(s, b):
        where = (s, slice(None), pl.ds(pl.multiple_of(b * groups, 8), groups))
        x = recv[where].reshape(tokens, feat)
        normed = split(layer_norm(x, gain_attn[...]))
        qkv = dot3(normed, (wq[0], wq[1]))
        q = qkv[:, :feat] * scale
        k = split(qkv[:, feat : 2 * feat])
        v = split(qkv[:, 2 * feat :])
        mixed = jnp.zeros((tokens, feat), F32)
        for h in range(HEADS):
            mine = lane_head == h
            scores = dot3(split(jnp.where(mine, q, 0.0)), k, ((1,), (1,))) + bias[h]
            expd = jnp.exp(scores - jnp.max(scores, axis=-1, keepdims=True))
            total = jnp.sum(expd, axis=-1, keepdims=True)
            mixed = mixed + jnp.where(mine, dot3(split(expd), v) / total, 0.0)
        after = x + dot3(split(mixed), (wp[0], wp[1]))
        hidden = gelu(dot3(split(layer_norm(after, gain_mlp[...])), (wu[0], wu[1])))
        result = after + dot3(split(hidden), (wd[0], wd[1]))
        done[where] = result.reshape(members, groups, feat)

    def process(s, carry):
        def await_one(step, inner):
            arrival(s, other(step)).wait_recv()
            return inner

        lax.fori_loop(1, members, await_one, 0)

        def work(b, inner):
            block(s, b)
            return inner

        lax.fori_loop(0, share // groups, work, 0)

        def send(step, inner):
            back(s, other(step)).start()
            return inner

        lax.fori_loop(1, members, send, 0)
        own(s).start()
        return carry

    lax.fori_loop(0, STAGES, process, 0)

    def finish(s, carry):
        def each(step, inner):
            member = other(step)
            go(s, member).wait_send()
            back(s, member).wait_send()
            back_arrival(s, member).wait_recv()
            return inner

        lax.fori_loop(1, members, each, 0)
        own(s).wait()
        return carry

    lax.fori_loop(0, STAGES, finish, 0)
    for index in range(8):
        @pl.when(plan[index][0])
        def _(index=index):
            halo_copy(index).wait_send()


def per_device(
    latent, w_small, w_large, gain_embed, gain_attn, w_qkv, pos_bias, w_proj, gain_mlp, w_up, w_down
):
    row_count = lax.axis_size("rows")
    col_count = lax.axis_size("cols")
    samples, rows, cols, chan = latent.shape
    tile_rows, tile_cols = rows // 2, cols // 2
    feat = gain_embed.shape[0]
    half = feat // 2
    members = pos_bias.shape[1]
    phases = row_count // (members // col_count)
    share = tile_rows * tile_cols // STAGES // members
    tokens = members * max(8, min(share, 256 // members))
    pixels = pltpu.VMEM((2, tile_rows + 1, tile_cols, 2 * chan), BF16)
    exchange = pltpu.VMEM((STAGES, members, share, feat), F32)
    dma = pltpu.SemaphoreType.DMA
    vmem = pl.BlockSpec(memory_space=pltpu.VMEM)
    halves = lambda *shape: pltpu.VMEM((2,) + shape, BF16)
    out = pl.pallas_call(
        functools.partial(block_kernel, (row_count, col_count, members, phases)),
        name="crossformer_block",
        out_shape=jax.ShapeDtypeStruct((tile_rows * tile_cols, feat), F32),
        in_specs=[vmem] * 11,
        out_specs=pl.BlockSpec(memory_space=pl.ANY),
        scratch_shapes=[
            pixels, pixels, pixels, pixels,
            halves(2, 2 * chan, feat),
            halves(2, 2 * chan, half),
            halves(4, 2 * chan, half),
            halves(*w_qkv.shape),
            halves(*w_proj.shape),
            halves(*w_up.shape),
            halves(*w_down.shape),
            pltpu.VMEM((HEADS, tokens, tokens), F32),
            exchange, exchange, exchange,
            pltpu.VMEM((2, cols, chan), F32),
            pltpu.VMEM((2, rows + 16, chan), F32),
            pltpu.VMEM((4, 8, chan), F32),
            pltpu.VMEM((2, rows, chan), F32),
            dma((8,)), dma((8,)),
            dma((STAGES, members)), dma((STAGES, members)),
            dma((STAGES, members)), dma((STAGES, members)),
        ],
        compiler_params=pltpu.CompilerParams(
            collective_id=0, has_side_effects=True, vmem_limit_bytes=67043328
        ),
    )(
        latent[0], w_small, w_large, gain_embed[None], gain_attn[None], w_qkv, pos_bias, w_proj,
        gain_mlp[None], w_up, w_down,
    )
    return out.reshape(samples, tile_rows, tile_cols, feat)


def solution(mesh):
    in_specs = (P(None, "rows", "cols", None),) + (P(),) * 10
    out_specs = P(None, "rows", "cols", None)
    return jax.shard_map(
        per_device, mesh=mesh, in_specs=in_specs, out_specs=out_specs, check_vma=False
    )
```

time: 382 us -> 113 us (0.30); the launches traced: 375 us -> 113 us
  blocking collectives: 112 us -> 0 us
  Pallas kernels: 0 us -> 110 us
  matrix products: 98.6 us -> 0 us
  local copies, waits for them, and re-layouts: 82.9 us -> 3.13 us
  waiting for transfers between devices: 46.8 us -> 0 us
  other arithmetic: 20.2 us -> 0 us
  starting transfers between devices: 13.9 us -> 0 us
    all_to_all x3 -> x0, blocking collectives: 112 us -> none  [the longest x1 50.4 us: to_tiles(): lax.all_to_all(lax.all_to_all(ordered.reshape(row_count, col_count, slots...]
    pallas_call x0 -> x1, Pallas kernels: none -> 110 us  [per_device(): pl.pallas_call(functools.partial(block_kernel, (row_count, col_count, mem...]
    dot_general x11 -> x0, matrix products: 98.6 us -> none  [the longest x4 46.9 us: matmul(): jnp.dot(left, right, precision=lax.Precision.HIGHEST, preferred_element_t...]
    all_to_all x1 -> x0, waiting for transfers between devices: 45.3 us -> none  [to_groups(): lax.all_to_all(lax.all_to_all(flat.reshape(row_count, col_count, slots, f...]
    squeeze x4 -> x0, local copies, waits for them, and re-layouts: 27.2 us -> none  [the longest x2 11.2 us: attend(): split[:, :, 1]]
    slice x3 -> x0, local copies, waits for them, and re-layouts: 16.1 us -> none  [the longest x1 15 us: per_device(): padded_blocks[:, row_block:row_block + rows_tile, :, col_block:col_block...]
    reshape x3 -> x0, local copies, waits for them, and re-layouts: 15.9 us -> none  [the longest x1 7.22 us: per_device(): padded.reshape(samples, rows_tile + 1, 2, cols_tile + 1, 2, channels)]
    reduce_sum x5 -> x0, other arithmetic: 10.3 us -> none  [the longest x1 5.5 us: attend(): probs = expd / jnp.sum(expd, axis=-1, keepdims=True)]
  transfers between devices with their start and end apart: 5 -> 0, of which waited for: 3 -> 0; matrix products, arithmetic and copies ran while one was open for 2% -> 0% of each run, Pallas kernels for 0% -> 0%
where the time goes in v1:
time: 113 us
  Pallas kernels  110 us (97%)
  local copies, waits for them, and re-layouts  3.13 us (3%)
    pallas_call x1, Pallas kernels, per_device(): pl.pallas_call(functools.partial(block_kernel, (row_count, col_count, mem...  110 us
    unnamed x1, local copies, waits for them, and re-layouts  3.13 us

profile of v1, /device:TPU:0, one launch (start us, length us, event | category | flops | bytes accessed | tf_op | source)
XLA Modules:
  0.0 113.0 jit_solution(18120099805997028300)
XLA Ops:
  0.0 109.8 %crossformer_block.1 = f32[2048,256]{1,0:T(8,128)} custom-call(f32[64,128,128]{2,1,0:T(8,128)} %bitcast.6, f32[512,128]{1,0:T(8,128)} %w_small.1, f32[2048,128]{1,0:T(8,128)} %w_large.1, f32[1,256]{1,0:T(1,128)} %bitcast.7, f32[1,256]{1,0:T(1,128)} %bitcast.8, f32[256,768]{1,0:T(8,128)} %w_qkv.1, f32[8,16,16]{2,1,0:T(8,128)} %pos_bias.1, f32[256,256]{1,0:T(8,128)} %w_proj.1, ...), custom_call_target="tpu_custom_call" | custom-call | tf_op jit(solution)/shard_map/crossformer_block/pallas_call | solution.py:335
  109.8 3.1 %copy.13 = f32[1,32,64,256]{3,2,1,0:T(8,128)} copy(f32[1,32,64,256]{3,2,1,0:T(8,128)} %bitcast.5) | data formatting | bytes 4194304

commit v2 on v1

--- a/solution.py
+++ b/solution.py
@@ -43,12 +43,15 @@
 
 def block_kernel(
     sizes,
-    lat, w_small, w_large, gain_embed, gain_attn, w_qkv, pos_bias, w_proj, gain_mlp, w_up, w_down,
-    out,
-    eo_hi, eo_lo, oe_hi, oe_lo, wc, we, wo, wq, wp, wu, wd, bias,
-    emb, recv, done, row_halo, col_halo, corner_halo, col_edge,
-    halo_send, halo_recv, go_send, go_recv, back_send, back_recv,
+    *refs,
 ):
+    inputs, out, loaded = refs[:11], refs[11], refs[12:23]
+    lat, w_small, w_large, gain_embed, gain_attn, w_qkv, pos_bias, w_proj, gain_mlp, w_up, w_down = loaded
+    (
+        eo_hi, eo_lo, oe_hi, oe_lo, wc, we, wo, wq, wp, wu, wd, bias,
+        emb, recv, done, row_halo, col_halo, corner_halo, col_edge,
+        halo_send, halo_recv, go_send, go_recv, back_send, back_recv, load_sem,
+    ) = refs[23:]
     row_count, col_count, members, phases = sizes
     rows, cols, chan = lat.shape
     tile_rows, tile_cols = rows // 2, cols // 2
@@ -89,6 +92,12 @@
             def _(dr=dr, dc=dc):
                 pl.semaphore_signal(barrier, inc=1, device_id=(r + dr, c + dc), device_id_type=MESH)
 
+    def load(index):
+        return pltpu.make_async_copy(inputs[index], loaded[index], load_sem.at[index])
+
+    for index in range(11):
+        load(index).start()
+    load(0).wait()
     col_edge[0] = lat[:, 0, :]
     col_edge[1] = lat[:, cols - 1, :]
     number = lambda flag: jnp.where(flag, 1, 0)
@@ -120,6 +129,40 @@
         def _(index=index):
             halo_copy(index).start()
 
+    first_row = lax.broadcasted_iota(jnp.int32, (tile_cols, 1), 0) == 0
+    last_row = lax.broadcasted_iota(jnp.int32, (tile_cols, 1), 0) == tile_cols - 1
+
+    def lay(hi, lo, t, left, right):
+        b, a = t % 2, t // 2
+        hi[b, a, :, :chan], lo[b, a, :, :chan] = split(left)
+        hi[b, a, :, chan:], lo[b, a, :, chan:] = split(right)
+
+    def columns(source):
+        return source[pl.ds(0, tile_cols, stride=2), :], source[pl.ds(1, tile_cols, stride=2), :]
+
+    def build_inner(t, source):
+        lay(eo_hi, eo_lo, t, *columns(source))
+
+    def build_outer(t, source):
+        even, odd = columns(source)
+        before = jnp.where(first_row, col_halo[0, pl.ds(t + 7, 1)], pltpu.roll(odd, 1, 0))
+        after = jnp.where(last_row, col_halo[1, pl.ds(t + 7, 1)], pltpu.roll(even, tile_cols - 1, 0))
+        lay(oe_hi, oe_lo, t, before, after)
+
+    def inner_line(t, carry):
+        build_inner(t, lat.at[t - 1])
+        return carry
+
+    def outer_line(t, carry):
+        build_outer(t, lat.at[t - 1])
+        return carry
+
+    def both_lines(t, carry):
+        return outer_line(t, inner_line(t, carry))
+
+    lax.fori_loop(1, 2 * stage_rows + 2, inner_line, 0)
+    load(1).wait()
+    load(2).wait()
     def keep(ref, index, values):
         ref[(0,) + index], ref[(1,) + index] = split(values)
 
@@ -148,22 +191,12 @@
         col_halo[side, 7] = corner_halo[side, row]
         col_halo[side, 8 + rows] = corner_halo[2 + side, row]
 
-    first_row = lax.broadcasted_iota(jnp.int32, (tile_cols, 1), 0) == 0
-    last_row = lax.broadcasted_iota(jnp.int32, (tile_cols, 1), 0) == tile_cols - 1
-
-    def build(t, source):
-        even = source[pl.ds(0, tile_cols, stride=2), :]
-        odd = source[pl.ds(1, tile_cols, stride=2), :]
-        before = jnp.where(first_row, col_halo[0, pl.ds(t + 7, 1)], pltpu.roll(odd, 1, 0))
-        after = jnp.where(last_row, col_halo[1, pl.ds(t + 7, 1)], pltpu.roll(even, tile_cols - 1, 0))
-        b, a = t % 2, t // 2
-        for hi, lo, left, right in ((eo_hi, eo_lo, even, odd), (oe_hi, oe_lo, before, after)):
-            hi[b, a, :, :chan], lo[b, a, :, :chan] = split(left)
-            hi[b, a, :, chan:], lo[b, a, :, chan:] = split(right)
-
-    build(0, row_halo.at[0])
-    build(1, lat.at[0])
-    build(rows + 1, row_halo.at[1])
+    lax.fori_loop(1, 2 * stage_rows + 2, outer_line, 0)
+    for t, side in ((0, 0), (rows + 1, 1)):
+        build_inner(t, row_halo.at[side])
+        build_outer(t, row_halo.at[side])
+    for index in range(3, 11):
+        load(index).wait()
 
     def go(s, member):
         rank = place(member)
@@ -197,13 +230,6 @@
         return pltpu.make_async_copy(done.at[s, me], home(s, me), back_recv.at[s, me])
 
     def embed(s, carry):
-        def line(t, inner):
-            build(t, lat.at[t - 1])
-            return inner
-
-        first = 2 * stage_rows * s + 2
-        lax.fori_loop(first, jnp.minimum(first + 2 * stage_rows, rows + 1), line, 0)
-
         def taps(hi, lo, p):
             where = (p % 2, pl.ds(stage_rows * s + p // 2, stage_rows))
             return tuple(ref[where].reshape(stage_tokens, 2 * chan) for ref in (hi, lo))
@@ -217,13 +243,17 @@
             thin = thin + dot3(taps(oe_hi, oe_lo, p), pair(wo, p))
         joined = jnp.concatenate([wide[:, :half], wide[:, half:] + thin], axis=-1)
         emb[s] = layer_norm(joined, gain_embed[...]).reshape(members, share, feat)
-        recv[s, me] = emb[s, me]
 
         def send(step, inner):
             go(s, other(step)).start()
             return inner
 
         lax.fori_loop(1, members, send, 0)
+        recv[s, me] = emb[s, me]
+        following = 2 * stage_rows * (s + 1) + 2
+        lax.fori_loop(
+            following, jnp.minimum(following + 2 * stage_rows, rows + 1), both_lines, 0
+        )
         return carry
 
     lax.fori_loop(0, STAGES, embed, 0)
@@ -330,15 +360,19 @@
     pixels = pltpu.VMEM((2, tile_rows + 1, tile_cols, 2 * chan), BF16)
     exchange = pltpu.VMEM((STAGES, members, share, feat), F32)
     dma = pltpu.SemaphoreType.DMA
-    vmem = pl.BlockSpec(memory_space=pltpu.VMEM)
+    inputs = (
+        latent[0], w_small, w_large, gain_embed[None], gain_attn[None], w_qkv, pos_bias, w_proj,
+        gain_mlp[None], w_up, w_down,
+    )
     halves = lambda *shape: pltpu.VMEM((2,) + shape, BF16)
     out = pl.pallas_call(
         functools.partial(block_kernel, (row_count, col_count, members, phases)),
         name="crossformer_block",
         out_shape=jax.ShapeDtypeStruct((tile_rows * tile_cols, feat), F32),
-        in_specs=[vmem] * 11,
+        in_specs=[pl.BlockSpec(memory_space=pltpu.HBM)] * 11,
         out_specs=pl.BlockSpec(memory_space=pl.ANY),
-        scratch_shapes=[
+        scratch_shapes=[pltpu.VMEM(array.shape, F32) for array in inputs]
+        + [
             pixels, pixels, pixels, pixels,
             halves(2, 2 * chan, feat),
             halves(2, 2 * chan, half),
@@ -356,14 +390,12 @@
             dma((8,)), dma((8,)),
             dma((STAGES, members)), dma((STAGES, members)),
             dma((STAGES, members)), dma((STAGES, members)),
+            dma((11,)),
         ],
         compiler_params=pltpu.CompilerParams(
             collective_id=0, has_side_effects=True, vmem_limit_bytes=67043328
         ),
-    )(
-        latent[0], w_small, w_large, gain_embed[None], gain_attn[None], w_qkv, pos_bias, w_proj,
-        gain_mlp[None], w_up, w_down,
-    )
+    )(*inputs)
     return out.reshape(samples, tile_rows, tile_cols, feat)
 
 

time: 113 us -> 110 us (0.973)
  Pallas kernels: 110 us -> 106 us
    pallas_call x1, Pallas kernels: 110 us -> 106 us  [per_device(): pl.pallas_call(functools.partial(block_kernel, (row_count, col_count, mem...]
where the time goes in v2:
time: 110 us
  Pallas kernels  106 us (96%)
  local copies, waits for them, and re-layouts  3.13 us (3%)
    pallas_call x1, Pallas kernels, per_device(): pl.pallas_call(functools.partial(block_kernel, (row_count, col_count, mem...  106 us
    unnamed x1, local copies, waits for them, and re-layouts  3.13 us

profile of v2, /device:TPU:0, one launch (start us, length us, event | category | flops | bytes accessed | tf_op | source)
XLA Modules:
  0.0 109.6 jit_solution(2720477329063367481)
XLA Ops:
  0.0 106.4 %crossformer_block.1 = f32[2048,256]{1,0:T(8,128)} custom-call(f32[64,128,128]{2,1,0:T(8,128)} %bitcast.6, f32[512,128]{1,0:T(8,128)} %refs_1_.1, f32[2048,128]{1,0:T(8,128)} %refs_2_.1, f32[1,256]{1,0:T(1,128)} %bitcast.7, f32[1,256]{1,0:T(1,128)} %bitcast.8, f32[256,768]{1,0:T(8,128)} %refs_5_.1, f32[8,16,16]{2,1,0:T(8,128)} %refs_6_.1, ...), custom_call_target="tpu_custom_call" | custom-call | tf_op jit(solution)/shard_map/crossformer_block/pallas_call | solution.py:368
  106.4 3.1 %copy.13 = f32[1,32,64,256]{3,2,1,0:T(8,128)} copy(f32[1,32,64,256]{3,2,1,0:T(8,128)} %bitcast.5) | data formatting | bytes 4194304

commit v3 on v2

--- a/solution.py
+++ b/solution.py
@@ -73,7 +73,11 @@
         return (member // col_count) * phases + core, lax.rem(member, col_count)
 
     def other(step):
-        return lax.rem(me + step, members)
+        per = members // col_count
+        g = (step - 1) // per
+        dk = lax.rem(step, per)
+        dc = lax.rem(col_count // 2 + (g + 1) // 2 * (2 * lax.rem(g, 2) - 1) + col_count, col_count)
+        return lax.rem(me // col_count + dk, per) * col_count + lax.rem(c + dc, col_count)
 
     barrier = pltpu.get_barrier_semaphore()
 

time: 110 us -> 108 us (0.982)
    pallas_call x1, Pallas kernels: 106 us -> 105 us  [per_device(): pl.pallas_call(functools.partial(block_kernel, (row_count, col_count, mem...]
where the time goes in v3:
time: 108 us
  Pallas kernels  105 us (97%)
  local copies, waits for them, and re-layouts  3.13 us (3%)
    pallas_call x1, Pallas kernels, per_device(): pl.pallas_call(functools.partial(block_kernel, (row_count, col_count, mem...  105 us
    unnamed x1, local copies, waits for them, and re-layouts  3.13 us

profile of v3, /device:TPU:0, one launch (start us, length us, event | category | flops | bytes accessed | tf_op | source)
XLA Modules:
  0.0 107.8 jit_solution(1182636126661883607)
XLA Ops:
  0.0 104.7 %crossformer_block.1 = f32[2048,256]{1,0:T(8,128)} custom-call(f32[64,128,128]{2,1,0:T(8,128)} %bitcast.6, f32[512,128]{1,0:T(8,128)} %refs_1_.1, f32[2048,128]{1,0:T(8,128)} %refs_2_.1, f32[1,256]{1,0:T(1,128)} %bitcast.7, f32[1,256]{1,0:T(1,128)} %bitcast.8, f32[256,768]{1,0:T(8,128)} %refs_5_.1, f32[8,16,16]{2,1,0:T(8,128)} %refs_6_.1, ...), custom_call_target="tpu_custom_call" | custom-call | tf_op jit(solution)/shard_map/crossformer_block/pallas_call | solution.py:372
  104.7 3.1 %copy.13 = f32[1,32,64,256]{3,2,1,0:T(8,128)} copy(f32[1,32,64,256]{3,2,1,0:T(8,128)} %bitcast.5) | data formatting | bytes 4194304
